TPU v7x, 32 devices: a whole 2x2x4 slice. The times are simulated.
32 devices in a mesh: clips: 2 (over y), seq: 4 (over z), tp: 2 (over x), dp: 2 (over core).
Axes of the slice: x: 2, y: 2, z: 4, core: 2. Of those that a mesh axis runs over, the one named last changes fastest.
Arguments:
- video_query: bfloat16 [4, 512, 4096], P(('clips', 'dp'), 'seq', 'tp'), parts along dimension 0, may hold values from -384 to 384
- video_key: bfloat16 [4, 512, 4096], P(('clips', 'dp'), 'seq', 'tp'), parts along dimension 0, may hold values from -384 to 384
- video_value: bfloat16 [4, 512, 4096], P(('clips', 'dp'), 'seq', 'tp'), parts along dimension 0, may hold values from -6 to 6
- cross_query: bfloat16 [4, 512, 2048], P(('clips', 'dp'), 'seq', 'tp'), parts along dimension 0, may hold values from -384 to 384
- audio_key: bfloat16 [4, 32, 2048], P(('clips', 'dp'), 'seq', 'tp'), parts along dimension 0, may hold values from -384 to 384
- audio_value: bfloat16 [4, 32, 2048], P(('clips', 'dp'), 'seq', 'tp'), parts along dimension 0, may hold values from -6 to 6
- audio_query: bfloat16 [4, 32, 2048], P(('clips', 'dp'), 'seq', 'tp'), parts along dimension 0, may hold values from -384 to 384
- cross_key: bfloat16 [4, 512, 2048], P(('clips', 'dp'), 'seq', 'tp'), parts along dimension 0, may hold values from -384 to 384
- cross_value: bfloat16 [4, 512, 2048], P(('clips', 'dp'), 'seq', 'tp'), parts along dimension 0, may hold values from -6 to 6
- audio_input: bfloat16 [4, 32, 2048], P(('clips', 'dp'), 'seq'), parts along dimension 0, may hold values from -0.29882812 to 0.29882812
- norm_gain: float32 [2048], replicated, may hold values from 0.1 to 1.9
- up_weight: bfloat16 [2048, 8192], P('tp', 'seq'), may hold values from -0.125 to 0.125
- down_weight: bfloat16 [8192, 2048], P('seq', 'tp'), may hold values from -0.0625 to 0.0625
Outputs:
- video_mixed: bfloat16 [4, 512, 4096], P(('clips', 'dp'), 'seq', 'tp'), parts along dimension 0
- video_heard: bfloat16 [4, 512, 2048], P(('clips', 'dp'), 'seq', 'tp'), parts along dimension 0
- audio_seen: bfloat16 [4, 32, 2048], P(('clips', 'dp'), 'seq', 'tp'), parts along dimension 0
- audio_mlp: bfloat16 [4, 32, 2048], P(('clips', 'dp'), 'seq', 'tp'), parts along dimension 0
There are 2 independent parts, one for each index of `clips`. A program takes and returns all parts, laid end to end along the dimension named above; an argument that names none is the same for every part. Nothing has to cross between parts.
All inputs are finite; a program needn't handle non-finite values.
Results may differ from a plain program's by a relative error of at most 0.013.
Values may be sent and summed in bfloat16 or wider, within the bound.
A program may use at most 64 MiB of HBM per device.

v0:
```python
import math
import jax
import jax.numpy as jnp
from jax import lax
from jax.sharding import PartitionSpec as P

VHEAD = 128
CHEAD = 64


def attend_rows(queries, keys_in, values_in, head_count):
    head_size = queries.shape[1] // head_count
    query_heads = queries.reshape(queries.shape[0], head_count, head_size)
    key_heads = keys_in.reshape(keys_in.shape[0], head_count, head_size)
    value_heads = values_in.reshape(values_in.shape[0], head_count, head_size)
    scores = jnp.einsum(
        "qhd,khd->qhk", query_heads, key_heads, preferred_element_type=jnp.float32
    ) / math.sqrt(head_size)
    peak_value = jnp.max(scores, axis=2, keepdims=True)
    weights = jnp.exp(scores - peak_value)
    totals = jnp.sum(weights, axis=2)
    weighted = jnp.einsum(
        "qhk,khd->qhd",
        weights.astype(jnp.bfloat16),
        value_heads,
        preferred_element_type=jnp.float32,
    )
    result = weighted / totals[:, :, None]
    return result.reshape(queries.shape[0], head_count * head_size).astype(jnp.bfloat16)


def attend(queries, keys_in, values_in, head_count):
    row_total = queries.shape[0]
    block_rows = 512 if row_total % 512 == 0 else row_total
    pieces = queries.reshape(row_total // block_rows, block_rows, queries.shape[1])
    result = lax.map(
        lambda row_piece: attend_rows(row_piece, keys_in, values_in, head_count), pieces
    )
    return result.reshape(row_total, queries.shape[1])


def video_self(queries, keys_in, values_in):
    seq_count = lax.axis_size("seq")
    local_heads = queries.shape[1] // VHEAD
    dest_heads = max(local_heads // seq_count, 1)
    blocks = seq_count * dest_heads // local_heads
    groups = local_heads // dest_heads
    group_width = dest_heads * VHEAD
    token_count = queries.shape[0]
    block_tokens = token_count // blocks

    def spread(tensor):
        shaped = tensor.reshape(token_count, groups, group_width).transpose(1, 0, 2)
        shaped = jnp.broadcast_to(shaped[:, None], (groups, blocks, token_count, group_width))
        return shaped.reshape(seq_count, token_count, group_width)

    shaped = queries.reshape(blocks, block_tokens, groups, group_width).transpose(2, 0, 1, 3)
    own_queries = lax.all_to_all(
        shaped.reshape(seq_count, block_tokens, group_width),
        "seq",
        split_axis=0,
        concat_axis=0,
        tiled=True,
    )
    keys_all = lax.all_to_all(spread(keys_in), "seq", split_axis=0, concat_axis=0, tiled=True)
    values_all = lax.all_to_all(spread(values_in), "seq", split_axis=0, concat_axis=0, tiled=True)
    keys_all = keys_all.reshape(-1, group_width)
    values_all = values_all.reshape(-1, group_width)
    own_queries = own_queries.reshape(-1, group_width)
    attended = attend(own_queries, keys_all, values_all, dest_heads)
    returned = lax.all_to_all(
        attended.reshape(seq_count, block_tokens, group_width),
        "seq",
        split_axis=0,
        concat_axis=0,
        tiled=True,
    )
    returned = returned.reshape(groups, blocks, block_tokens, group_width).transpose(1, 2, 0, 3)
    return returned.reshape(token_count, groups * group_width)


def audio_listen(queries, keys_in, values_in, head_count):
    head_size = queries.shape[1] // head_count
    query_heads = queries.reshape(queries.shape[0], head_count, head_size)
    key_heads = keys_in.reshape(keys_in.shape[0], head_count, head_size)
    value_heads = values_in.reshape(values_in.shape[0], head_count, head_size)
    scores = jnp.einsum(
        "qhd,khd->qhk", query_heads, key_heads, preferred_element_type=jnp.float32
    ) / math.sqrt(head_size)
    local_peak = jnp.max(scores, axis=2)
    peak_value = lax.pmax(local_peak, "seq")
    weights = jnp.exp(scores - peak_value[:, :, None])
    totals = jnp.sum(weights, axis=2)
    weighted = jnp.einsum(
        "qhk,khd->qhd",
        weights.astype(jnp.bfloat16),
        value_heads,
        preferred_element_type=jnp.float32,
    )
    totals, weighted = (totals, weighted.reshape(queries.shape[0], head_count * head_size))
    totals, weighted = (
        lax.psum_scatter(totals, "seq", scatter_dimension=0, tiled=True),
        lax.psum_scatter(weighted, "seq", scatter_dimension=0, tiled=True),
    )
    return (weighted / jnp.repeat(totals, head_size, axis=1)).astype(jnp.bfloat16)


def audio_block(audio_rows, audio_seen, norm_gain, up_weight, down_weight):
    features = lax.all_gather(audio_seen, "tp", axis=1, tiled=True)
    residual = audio_rows.astype(jnp.float32) + features.astype(jnp.float32)
    scale_factor = lax.rsqrt(jnp.mean(residual * residual, axis=1, keepdims=True) + 1e-06)
    normed = (residual * scale_factor * norm_gain).astype(jnp.bfloat16)
    slice_width = up_weight.shape[0]
    own_features = lax.dynamic_slice_in_dim(
        normed, lax.axis_index("tp") * slice_width, slice_width, 1
    )
    partial_sum = jnp.dot(
        lax.all_gather(own_features, "seq", axis=0, tiled=True),
        up_weight,
        preferred_element_type=jnp.float32,
    )
    hidden = jax.nn.gelu(lax.psum(partial_sum, "tp")).astype(jnp.bfloat16)
    return lax.psum_scatter(
        jnp.dot(hidden, down_weight, preferred_element_type=jnp.float32),
        "seq",
        scatter_dimension=0,
        tiled=True,
    ).astype(jnp.bfloat16)


def body(
    video_query,
    video_key,
    video_value,
    cross_query,
    audio_key,
    audio_value,
    audio_query,
    cross_key,
    cross_value,
    audio_input,
    norm_gain,
    up_weight,
    down_weight,
):
    mixed_list, heard_list, seen_list, output_list = ([], [], [], [])
    cross_heads = cross_query.shape[2] // CHEAD
    mixed_list.append(video_self(video_query[0], video_key[0], video_value[0]))
    gathered_query = lax.all_gather(audio_query[0], "seq", axis=0, tiled=True)
    gathered_key = lax.all_gather(audio_key[0], "seq", axis=0, tiled=True)
    gathered_value = lax.all_gather(audio_value[0], "seq", axis=0, tiled=True)
    heard_list.append(attend(cross_query[0], gathered_key, gathered_value, cross_heads))
    audio_seen = audio_listen(gathered_query, cross_key[0], cross_value[0], cross_heads)
    seen_list.append(audio_seen)
    output_list.append(audio_block(audio_input[0], audio_seen, norm_gain, up_weight, down_weight))
    return (
        jnp.stack(mixed_list),
        jnp.stack(heard_list),
        jnp.stack(seen_list),
        jnp.stack(output_list),
    )


def solution(mesh):
    placed = (
        P(("clips", "dp"), "seq", "tp"),
        P(("clips", "dp"), "seq", "tp"),
        P(("clips", "dp"), "seq", "tp"),
        P(("clips", "dp"), "seq", "tp"),
        P(("clips", "dp"), "seq", "tp"),
        P(("clips", "dp"), "seq", "tp"),
        P(("clips", "dp"), "seq", "tp"),
        P(("clips", "dp"), "seq", "tp"),
        P(("clips", "dp"), "seq", "tp"),
        P(("clips", "dp"), "seq", None),
        P(),
        P("tp", "seq"),
        P("seq", "tp"),
    )
    return jax.shard_map(
        body,
        mesh=mesh,
        in_specs=placed,
        out_specs=(
            P(("clips", "dp"), "seq", "tp"),
            P(("clips", "dp"), "seq", "tp"),
            P(("clips", "dp"), "seq", "tp"),
            P(("clips", "dp"), "seq", "tp"),
        ),
        check_vma=False,
    )
```

profile of v0, /device:TPU:0, one launch (start us, length us, event | category | flops | bytes accessed | tf_op | source)
XLA Modules:
  0.0 171.0 jit_solution(16451558797304456168)
XLA Ops:
  7.2 2.0 %copy.100 = bf16[1,16,4,8,512]{4,3,1,2,0:T(8,128)(2,1)} copy(bf16[1,16,4,8,512]{4,3,2,1,0:T(8,128)(2,1)} %bitcast.77) | data formatting | bytes 1048576 | tf_op jit(solution)/shard_map/reshape;squeeze | solution.py:57
  9.2 6.3 %all-to-all-start.1 = ((bf16[4,128,512]{2,1,0:T(8,128)(2,1)}), bf16[4,128,512]{2,1,0:T(8,128)(2,1)S(1)}, u32[]{:S(2)}, u32[]{:S(2)}) async-start(bf16[4,128,512]{2,1,0:T(8,128)(2,1)} %bitcast.69), calls=%async_computation.1 | async-start | bytes 1048576 | tf_op jit(solution)/shard_map/all_to_all | solution.py:58
  15.5 0.0 reduce-scatter.3.cloned.1.call-start
  15.5 1.2 copy.70
  16.7 1.1 copy.68
  17.8 0.0 copy-start.9
  17.8 0.0 copy-start.8
  17.9 17.8 %all-gather.2 = bf16[1,32,1024]{2,1,0:T(8,128)(2,1)S(1)} all-gather(bf16[1,8,1024]{2,1,0:T(8,128)(2,1)} %param.19), channel_id=4, replica_groups=mesh['clips'=2,'seq'=4,'tp'=2,'dp'=2] {'seq'}, dimensions={1}, use_global_device_ids=true | all-gather | bytes 81920 | tf_op jit(solution)/shard_map/all_gather | solution.py:149
  35.7 0.1 reshape.82
  35.8 0.3 fusion.57
  36.1 11.0 %pmax.7 = f32[32,16]{0,1:T(8,128)S(1)} all-reduce(f32[32,16]{0,1:T(8,128)S(1)} %get-tuple-element.56), channel_id=1, replica_groups=mesh['clips'=2,'seq'=4,'tp'=2,'dp'=2] {'seq'}, use_global_device_ids=true, to_apply=%region_5.6 | all-reduce | flops 512 | bytes 4096 | tf_op jit(solution)/shard_map/pmax | solution.py:91
  47.2 0.3 convolution_bitcast_fusion.1
  47.5 0.2 copy.71
  47.6 0.8 reshape.83
  48.4 0.0 reduce-scatter.3.cloned.1.call-update
  48.5 0.4 reshape_squeeze.15
  48.9 0.9 copy.102
  49.7 0.4 reshape_squeeze.17
  50.1 0.9 copy.101
  51.0 0.2 copy.65
  51.2 13.2 %all-gather = bf16[1,32,1024]{2,1,0:T(8,128)(2,1)S(1)} all-gather(bf16[1,8,1024]{2,1,0:T(8,128)(2,1)S(1)} %copy-done.6), channel_id=2, replica_groups=mesh['clips'=2,'seq'=4,'tp'=2,'dp'=2] {'seq'}, dimensions={1}, use_global_device_ids=true | all-gather | bytes 81920 | tf_op jit(solution)/shard_map/all_gather | solution.py:150
  64.4 0.1 reshape.79
  64.5 0.3 fusion.34
  64.8 0.1 copy.72
  64.9 0.6 dynamic-slice
  66.1 15.7 %all-reduce = f32[32,16]{1,0:T(8,128)S(1)} all-reduce(f32[32,16]{1,0:T(8,128)S(1)} %copy.72), channel_id=6, replica_groups=mesh['clips'=2,'seq'=4,'tp'=2,'dp'=2] {'seq'}, use_global_device_ids=true, to_apply=%region_8.9.clone | all-reduce | flops 512 | bytes 4096
  81.8 0.1 broadcast_in_dim.16
  81.9 0.1 reshape.84
  82.0 0.2 fusion.56
  82.2 0.1 fusion.32
  82.3 3.5 %all-to-all-start = ((bf16[4,128,512]{2,1,0:T(8,128)(2,1)}), bf16[4,128,512]{2,1,0:T(8,128)(2,1)S(1)}, u32[]{:S(2)}, u32[]{:S(2)}) async-start(bf16[4,128,512]{2,1,0:T(8,128)(2,1)} %bitcast.71), calls=%async_computation | async-start | bytes 1048576 | tf_op jit(solution)/shard_map/all_to_all | solution.py:65
  85.8 0.0 reduce-scatter.3.cloned.1.call-done
  85.8 0.8 divide_convert_fusion
  86.6 0.0 copy-start.4
  86.6 4.4 %all_gather.18 = bf16[8,2048]{1,0:T(8,128)(2,1)S(1)} all-gather(bf16[8,1024]{1,0:T(8,128)(2,1)S(1)} %divide_convert_fusion), channel_id=1, replica_groups=mesh['clips'=2,'seq'=4,'tp'=2,'dp'=2] {'tp'}, dimensions={1}, use_global_device_ids=true | all-gather | bytes 49152 | tf_op jit(solution)/shard_map/all_gather | solution.py:109
  91.0 0.1 multiply_reduce_fusion
  91.2 0.1 fusion.50
  91.2 13.9 %all_gather.19 = bf16[32,1024]{1,0:T(8,128)(2,1)S(1)} all-gather(bf16[8,1024]{1,0:T(8,128)(2,1)S(1)} %fusion.50), channel_id=1, replica_groups=mesh['clips'=2,'seq'=4,'tp'=2,'dp'=2] {'seq'}, dimensions={0}, use_global_device_ids=true | all-gather | bytes 81920 | tf_op jit(solution)/shard_map/all_gather | solution.py:118
  105.1 4.6 %all-to-all-start.2 = ((bf16[4,128,512]{2,1,0:T(8,128)(2,1)}), bf16[4,128,512]{2,1,0:T(8,128)(2,1)S(1)}, u32[]{:S(2)}, u32[]{:S(2)}) async-start(bf16[4,128,512]{2,1,0:T(8,128)(2,1)} %bitcast.70), calls=%async_computation.2 | async-start | bytes 1048576 | tf_op jit(solution)/shard_map/all_to_all | solution.py:66
  109.7 3.7 %fusion.58 = f32[32,2048]{1,0:T(8,128)} fusion(bf16[32,1024]{1,0:T(8,128)(2,1)S(1)} %all_gather.19, bf16[1024,2048]{1,0:T(8,128)(2,1)} %param.24), kind=kOutput, calls=%fused_computation.67 | convolution fusion | flops 134217728 | bytes 4521984 | tf_op jit(solution)/shard_map/dot_general | solution.py:117
  113.4 0.0 all-reduce.3.cloned.1.call-update
  113.5 0.1 reshape.77
  113.6 0.1 reshape_reshape.10
  113.7 0.7 bitcast_reduce_fusion
  114.5 1.9 %copy-done = f32[4,512,512]{2,1,0:T(8,128)} copy-done((f32[4,512,512]{2,1,0:T(8,128)}, f32[4,512,512]{2,1,0:T(8,128)S(1)}, u32[]{:S(2)}) %copy-start) | copy-done | bytes 4194328
  116.4 0.7 fusion.1
  117.1 7.5 %all-to-all-done.2 = bf16[4,128,512]{2,1,0:T(8,128)(2,1)S(1)} async-done(((bf16[4,128,512]{2,1,0:T(8,128)(2,1)}), bf16[4,128,512]{2,1,0:T(8,128)(2,1)S(1)}, u32[]{:S(2)}, u32[]{:S(2)}) %all-to-all-start.2) | async-done | bytes 524320 | tf_op jit(solution)/shard_map/all_to_all | solution.py:66
  124.6 0.1 reshape_reshape.11
  124.8 3.4 %fusion.17 = bf16[512,4,128]{2,0,1:T(8,128)(2,1)S(1)} fusion(f32[4,512,512]{2,1,0:T(8,128)} %copy-done, f32[512,4]{0,1:T(4,128)S(1)} %get-tuple-element.52, bf16[512,4,128]{2,1,0:T(4,128)(2,1)S(1)} %reshape_reshape.11, f32[512,4]{0,1:T(4,128)S(1)} %fusion.1), kind=kOutput, calls=%fused_computation.18 | convolution fusion | flops 272105472 | bytes 5259264 | tf_op jit(solution)/shard_map/while/body/eval_jaxpr/qhk,khd->qhd/dot_general | solution.py:22
  128.2 0.4 copy.63
  128.6 1.0 convert_element_type.56
  129.6 3.5 %all-to-all-start.3 = ((bf16[4,128,512]{2,1,0:T(8,128)(2,1)}), bf16[4,128,512]{2,1,0:T(8,128)(2,1)S(1)}, u32[]{:S(2)}, u32[]{:S(2)}) async-start(bf16[4,128,512]{2,1,0:T(8,128)(2,1)} %convert_element_type.56), calls=%async_computation.3 | async-start | bytes 1048576 | tf_op jit(solution)/shard_map/all_to_all | solution.py:71
  133.0 0.0 reduce-scatter.5.cloned.1.call-start
  133.1 5.3 %all-reduce.3.cloned.1.call-done = f32[32,2048]{1,0:T(8,128)} async-done(((f32[32,2048]{1,0:T(8,128)}), f32[32,2048]{1,0:T(8,128)}) %all-reduce.3.cloned.1.call-update) | async-done | bytes 262160 | tf_op jit(solution)/shard_map/psum | solution.py:122
  138.4 3.7 %fusion.38 = f32[32,1024]{1,0:T(8,128)} fusion(bf16[2048,1024]{1,0:T(8,128)(2,1)} %param.25, f32[32,2048]{1,0:T(8,128)} %all-reduce.3.cloned.1.call-done), kind=kOutput, calls=%fused_computation.41 | convolution fusion | flops 134807552 | bytes 4587520 | tf_op jit(solution)/shard_map/dot_general | solution.py:124
  142.1 0.0 reduce-scatter.5.cloned.1.call-update
  142.1 13.3 %all-gather.1 = bf16[1,32,1024]{2,1,0:T(8,128)(2,1)S(1)} all-gather(bf16[1,8,1024]{2,1,0:T(8,128)(2,1)S(1)} %copy-done.7), channel_id=3, replica_groups=mesh['clips'=2,'seq'=4,'tp'=2,'dp'=2] {'seq'}, dimensions={1}, use_global_device_ids=true | all-gather | bytes 81920 | tf_op jit(solution)/shard_map/all_gather | solution.py:151
  155.4 0.1 reshape.81
  155.6 0.3 fusion.11
  155.8 0.9 copy.74
  156.7 5.1 %reduce-scatter.5.cloned.1.call-done = f32[8,1024]{1,0:T(8,128)} async-done(((f32[32,1024]{1,0:T(8,128)}), f32[8,1024]{1,0:T(8,128)}) %reduce-scatter.5.cloned.1.call-update) | async-done | bytes 32784 | tf_op jit(solution)/shard_map/reduce_scatter | solution.py:123
  161.8 1.4 convert_bitcast_fusion
  163.2 0.3 copy.64
  163.5 1.0 copy.73
  (23 shorter events, 0.1 us)
Async XLA Ops:
  7.2 41.3 %copy-start.1 = (bf16[1,128,2048]{2,1,0:T(8,128)(2,1)S(1)}, bf16[1,128,2048]{2,1,0:T(8,128)(2,1)}, u32[]{:S(2)}) copy-start(bf16[1,128,2048]{2,1,0:T(8,128)(2,1)} %param.14) | copy-start | bytes 1572868
  7.2 42.6 %copy-start.2 = (bf16[1,128,2048]{2,1,0:T(8,128)(2,1)S(1)}, bf16[1,128,2048]{2,1,0:T(8,128)(2,1)}, u32[]{:S(2)}) copy-start(bf16[1,128,2048]{2,1,0:T(8,128)(2,1)} %param.15) | copy-start | bytes 1572868
  9.2 73.1 %all-to-all-start.1 = ((bf16[4,128,512]{2,1,0:T(8,128)(2,1)}), bf16[4,128,512]{2,1,0:T(8,128)(2,1)S(1)}, u32[]{:S(2)}, u32[]{:S(2)}) async-start(bf16[4,128,512]{2,1,0:T(8,128)(2,1)} %bitcast.69), calls=%async_computation.1 | async-start | bytes 1048576 | tf_op jit(solution)/shard_map/all_to_all | solution.py:58
  15.5 35.5 %copy-start.3 = (bf16[1,128,1024]{2,1,0:T(8,128)(2,1)S(1)}, bf16[1,128,1024]{2,1,0:T(8,128)(2,1)}, u32[]{:S(2)}) copy-start(bf16[1,128,1024]{2,1,0:T(8,128)(2,1)} %param.16) | copy-start | bytes 786436
  15.5 35.7 %copy-start.6 = (bf16[1,8,1024]{2,1,0:T(8,128)(2,1)S(1)}, bf16[1,8,1024]{2,1,0:T(8,128)(2,1)}, u32[]{:S(2)}) copy-start(bf16[1,8,1024]{2,1,0:T(8,128)(2,1)} %param.17) | copy-start | bytes 49156
  15.5 70.3 %reduce-scatter.3.cloned.1.call-start = ((), (), s32[]{:S(2)}) async-start(), calls=%async_computation.6 | async-start | bytes 163840 | tf_op jit(solution)/shard_map/reduce_scatter | solution.py:103
  17.8 47.0 %copy-start.9 = (u32[32]{0:T(128)S(1)}, u32[32]{0:T(128)}, u32[]{:S(2)}) copy-start(u32[32]{0:T(128)} %constant.75) | copy-start | bytes 388
  17.8 64.2 %copy-start.8 = (f32[2048]{0:T(1024)S(1)}, f32[2048]{0:T(1024)}, u32[]{:S(2)}) copy-start(f32[2048]{0:T(1024)} %param.23) | copy-start | bytes 24580
  47.6 43.4 %copy-start.5 = (bf16[1,8,2048]{2,1,0:T(8,128)(2,1)S(1)}, bf16[1,8,2048]{2,1,0:T(8,128)(2,1)}, u32[]{:S(2)}) copy-start(bf16[1,8,2048]{2,1,0:T(8,128)(2,1)} %param.22) | copy-start | bytes 98308
  82.3 22.8 %all-to-all-start = ((bf16[4,128,512]{2,1,0:T(8,128)(2,1)}), bf16[4,128,512]{2,1,0:T(8,128)(2,1)S(1)}, u32[]{:S(2)}, u32[]{:S(2)}) async-start(bf16[4,128,512]{2,1,0:T(8,128)(2,1)} %bitcast.71), calls=%async_computation | async-start | bytes 1048576 | tf_op jit(solution)/shard_map/all_to_all | solution.py:65
  86.6 27.9 %copy-start.4 = (bf16[8,1024]{1,0:T(8,128)(2,1)}, bf16[8,1024]{1,0:T(8,128)(2,1)S(1)}, u32[]{:S(2)}) copy-start(bf16[8,1024]{1,0:T(8,128)(2,1)S(1)} %divide_convert_fusion) | copy-start | bytes 49156
  105.1 19.5 %all-to-all-start.2 = ((bf16[4,128,512]{2,1,0:T(8,128)(2,1)}), bf16[4,128,512]{2,1,0:T(8,128)(2,1)S(1)}, u32[]{:S(2)}, u32[]{:S(2)}) async-start(bf16[4,128,512]{2,1,0:T(8,128)(2,1)} %bitcast.70), calls=%async_computation.2 | async-start | bytes 1048576 | tf_op jit(solution)/shard_map/all_to_all | solution.py:66
  109.7 28.7 %all-reduce.3.cloned.1.call-start = ((), (), s32[]{:S(2)}) async-start(), calls=%async_computation.7 | async-start | bytes 524288 | tf_op jit(solution)/shard_map/psum | solution.py:122
  114.5 1.9 %copy-start = (f32[4,512,512]{2,1,0:T(8,128)}, f32[4,512,512]{2,1,0:T(8,128)S(1)}, u32[]{:S(2)}) copy-start(f32[4,512,512]{2,1,0:T(8,128)S(1)} %get-tuple-element.53) | copy-start | bytes 12582916
  128.1 14.0 %copy-start.7 = (bf16[1,8,1024]{2,1,0:T(8,128)(2,1)S(1)}, bf16[1,8,1024]{2,1,0:T(8,128)(2,1)}, u32[]{:S(2)}) copy-start(bf16[1,8,1024]{2,1,0:T(8,128)(2,1)} %param.18) | copy-start | bytes 49156
  129.6 33.6 %all-to-all-start.3 = ((bf16[4,128,512]{2,1,0:T(8,128)(2,1)}), bf16[4,128,512]{2,1,0:T(8,128)(2,1)S(1)}, u32[]{:S(2)}, u32[]{:S(2)}) async-start(bf16[4,128,512]{2,1,0:T(8,128)(2,1)} %convert_element_type.56), calls=%async_computation.3 | async-start | bytes 1048576 | tf_op jit(solution)/shard_map/all_to_all | solution.py:71
  133.0 28.8 %reduce-scatter.5.cloned.1.call-start = ((), (), s32[]{:S(2)}) async-start(), calls=%async_computation.8 | async-start | bytes 163840 | tf_op jit(solution)/shard_map/reduce_scatter | solution.py:123
Sparse Core Ops, SparseCore 0:
  48.6 17.6 reduce-scatter.2
  113.6 24.7 all-reduce.2
  142.2 19.5 reduce-scatter.4
where the time goes:
time: 172 us; the launch traced here: 171 us
  blocking collectives  89.4 us (52%)
  starting transfers between devices  18 us (10%)
  waiting for transfers between devices  18 us (10%)
  local copies, waits for them, and re-layouts  15 us (9%)
  between operations  14.7 us (9%)
  matrix products  12.6 us (7%)
  other arithmetic  3.38 us (2%)
    all_gather x1, blocking collectives, body(): gathered_query = lax.all_gather(audio_query[0], 'seq', axis=0, tiled=True)  17.8 us
    unnamed x1, blocking collectives  15.7 us
    all_gather x1, blocking collectives, audio_block(): lax.all_gather(own_features, 'seq', axis=0, tiled=True)  13.9 us
    all_gather x1, blocking collectives, body(): gathered_value = lax.all_gather(audio_value[0], 'seq', axis=0, tiled=True)  13.3 us
    all_gather x1, blocking collectives, body(): gathered_key = lax.all_gather(audio_key[0], 'seq', axis=0, tiled=True)  13.2 us
    pmax x1, blocking collectives, audio_listen(): peak_value = lax.pmax(local_peak, 'seq')  11 us
    all_to_all x1, waiting for transfers between devices, video_self(): lax.all_to_all(spread(values_in), 'seq', split_axis=0, concat_axis=0, til...  7.52 us
    unnamed x27, local copies, waits for them, and re-layouts  6.86 us
  transfers between devices with their start and end apart: 7, of which 3 were waited for; matrix products, arithmetic and copies ran while one was open for 15% of the time, Pallas kernels for 0%

commit v1 on v0

--- a/solution.py
+++ b/solution.py
@@ -146,7 +146,12 @@
     mixed_list, heard_list, seen_list, output_list = ([], [], [], [])
     cross_heads = cross_query.shape[2] // CHEAD
     mixed_list.append(video_self(video_query[0], video_key[0], video_value[0]))
-    gathered_query = lax.all_gather(audio_query[0], "seq", axis=0, tiled=True)
+    ring = [audio_query[0]]
+    for hop in range(3):
+        ring.append(lax.ppermute(ring[-1], "seq", [(dev, (dev + 1) % 4) for dev in range(4)]))
+    gathered_query = jnp.roll(
+        jnp.concatenate(ring[::-1], axis=0), (lax.axis_index("seq") + 1) * ring[0].shape[0], axis=0
+    )
     gathered_key = lax.all_gather(audio_key[0], "seq", axis=0, tiled=True)
     gathered_value = lax.all_gather(audio_value[0], "seq", axis=0, tiled=True)
     heard_list.append(attend(cross_query[0], gathered_key, gathered_value, cross_heads))

time: 172 us -> 164 us (0.953)
  blocking collectives: 89.4 us -> 74.6 us
  starting transfers between devices: 18 us -> 21.5 us
  waiting for transfers between devices: 18 us -> 21.2 us
    all_gather x1 -> x0, blocking collectives: 17.8 us -> none  [body(): gathered_query = lax.all_gather(audio_query[0], 'seq', axis=0, tiled=True)]
    ppermute x0 -> x3, starting transfers between devices: none -> 6.05 us  [body(): lax.ppermute(ring[-1], 'seq', [(dev, (dev + 1) % 4) for dev in range(4)])]
    all_gather x1, blocking collectives: 13.2 us -> 17 us  [body(): gathered_key = lax.all_gather(audio_key[0], 'seq', axis=0, tiled=True)]
    ppermute x0 -> x3, waiting for transfers between devices: none -> 3.15 us  [body(): lax.ppermute(ring[-1], 'seq', [(dev, (dev + 1) % 4) for dev in range(4)])]
    all_to_all x1, starting transfers between devices: 6.35 us -> 3.86 us  [video_self(): lax.all_to_all(shaped.reshape(seq_count, block_tokens, group_width), 'seq...]
    unnamed x27 -> x34, local copies, waits for them, and re-layouts: 6.86 us -> 6.9 us
  transfers between devices with their start and end apart: 7 -> 10, of which waited for: 3 -> 4; matrix products, arithmetic and copies ran while one was open for 15% -> 17% of each run, Pallas kernels for 0% -> 0%
where the time goes in v1:
time: 164 us; the launch traced here: 163 us
  blocking collectives  74.6 us (45%)
  starting transfers between devices  21.5 us (13%)
  waiting for transfers between devices  21.2 us (13%)
  local copies, waits for them, and re-layouts  15 us (9%)
  between operations  14.8 us (9%)
  matrix products  12.6 us (8%)
  other arithmetic  3.38 us (2%)
    all_gather x1, blocking collectives, body(): gathered_key = lax.all_gather(audio_key[0], 'seq', axis=0, tiled=True)  17 us
    unnamed x1, blocking collectives  16.6 us
    all_gather x1, blocking collectives, audio_block(): lax.all_gather(own_features, 'seq', axis=0, tiled=True)  13.9 us
    all_gather x1, blocking collectives, body(): gathered_value = lax.all_gather(audio_value[0], 'seq', axis=0, tiled=True)  13.3 us
    pmax x1, blocking collectives, audio_listen(): peak_value = lax.pmax(local_peak, 'seq')  9.38 us
    all_to_all x1, waiting for transfers between devices, video_self(): lax.all_to_all(spread(values_in), 'seq', split_axis=0, concat_axis=0, til...  7 us
    unnamed x34, local copies, waits for them, and re-layouts  6.9 us
    ppermute x3, starting transfers between devices, body(): lax.ppermute(ring[-1], 'seq', [(dev, (dev + 1) % 4) for dev in range(4)])  6.05 us
  transfers between devices with their start and end apart: 10, of which 4 were waited for; matrix products, arithmetic and copies ran while one was open for 17% of the time, Pallas kernels for 0%

profile of v1, /device:TPU:0, one launch (start us, length us, event | category | flops | bytes accessed | tf_op | source)
XLA Modules:
  0.0 163.0 jit_solution(1676137985285470547)
XLA Ops:
  7.2 3.1 %collective-permute-start = (bf16[8,1024]{1,0:T(8,128)(2,1)}, bf16[8,1024]{1,0:T(8,128)(2,1)S(1)}, u32[]{:S(2)}, u32[]{:S(2)}) collective-permute-start(bf16[8,1024]{1,0:T(8,128)(2,1)} %bitcast.83), channel_id=1, source_target_pairs={{0,4},{4,8},{8,12},{12,0},{1,5},{5,9},{9,13},{13,1},{2,6},{6,10},{... | collective-permute-start | bytes 49160 | tf_op jit(solution)/shard_map/ppermute | solution.py:151
  10.3 1.9 %copy.100 = bf16[1,16,4,8,512]{4,3,1,2,0:T(8,128)(2,1)} copy(bf16[1,16,4,8,512]{4,3,2,1,0:T(8,128)(2,1)} %bitcast.80) | data formatting | bytes 1048576 | tf_op jit(solution)/shard_map/reshape;squeeze | solution.py:57
  12.2 3.9 %all-to-all-start.1 = ((bf16[4,128,512]{2,1,0:T(8,128)(2,1)}), bf16[4,128,512]{2,1,0:T(8,128)(2,1)S(1)}, u32[]{:S(2)}, u32[]{:S(2)}) async-start(bf16[4,128,512]{2,1,0:T(8,128)(2,1)} %bitcast.72), calls=%async_computation.1 | async-start | bytes 1048576 | tf_op jit(solution)/shard_map/all_to_all | solution.py:58
  16.0 1.2 copy.65
  17.2 2.1 %collective-permute-start.1 = (bf16[8,1024]{1,0:T(8,128)(2,1)S(1)}, bf16[8,1024]{1,0:T(8,128)(2,1)S(1)}, u32[]{:S(2)}, u32[]{:S(2)}) collective-permute-start(bf16[8,1024]{1,0:T(8,128)(2,1)S(1)} %collective-permute-done), channel_id=1, source_target_pairs={{0,4},{4,8},{8,12},{12,0},{1,5},{5,9},{9,13},{13,1},{2,6},{6,10},{... | collective-permute-start | bytes 49160 | tf_op jit(solution)/shard_map/ppermute | solution.py:151
  19.3 17.0 %all-gather = bf16[1,32,1024]{2,1,0:T(8,128)(2,1)S(1)} all-gather(bf16[1,8,1024]{2,1,0:T(8,128)(2,1)} %param.17), channel_id=2, replica_groups=mesh['clips'=2,'seq'=4,'tp'=2,'dp'=2] {'seq'}, dimensions={1}, use_global_device_ids=true | all-gather | bytes 81920 | tf_op jit(solution)/shard_map/all_gather | solution.py:155
  36.3 0.1 reshape.79
  36.5 0.9 collective-permute-start.2
  37.3 0.2 fusion.56
  37.5 1.1 copy.70
  38.7 0.0 copy-start.9
  38.7 0.2 copy.68
  38.9 3.1 %collective-permute-done.2 = bf16[8,1024]{1,0:T(8,128)(2,1)S(1)} collective-permute-done((bf16[8,1024]{1,0:T(8,128)(2,1)S(1)}, bf16[8,1024]{1,0:T(8,128)(2,1)S(1)}, u32[]{:S(2)}, u32[]{:S(2)}) %collective-permute-start.2) | collective-permute-done | bytes 16416 | tf_op jit(solution)/shard_map/ppermute | solution.py:151
  42.1 0.1 reshape.82
  42.3 0.3 fusion.57
  42.6 9.4 %pmax.7 = f32[32,16]{0,1:T(8,128)S(1)} all-reduce(f32[32,16]{0,1:T(8,128)S(1)} %get-tuple-element.56), channel_id=1, replica_groups=mesh['clips'=2,'seq'=4,'tp'=2,'dp'=2] {'seq'}, use_global_device_ids=true, to_apply=%region_5.6 | all-reduce | flops 512 | bytes 4096 | tf_op jit(solution)/shard_map/pmax | solution.py:91
  52.0 0.3 convolution_bitcast_fusion.1
  52.3 0.2 copy.71
  52.5 0.8 reshape.83
  53.2 0.0 reduce-scatter.3.cloned.1.call-update
  53.3 0.1 fusion.32
  53.3 0.4 reshape_squeeze.15
  53.7 0.9 copy.102
  54.6 0.4 reshape_squeeze.17
  55.0 0.9 copy.101
  55.9 0.6 dynamic-slice
  57.1 0.3 fusion.34
  57.4 0.1 copy.72
  57.5 16.6 %all-reduce = f32[32,16]{1,0:T(8,128)S(1)} all-reduce(f32[32,16]{1,0:T(8,128)S(1)} %copy.72), channel_id=5, replica_groups=mesh['clips'=2,'seq'=4,'tp'=2,'dp'=2] {'seq'}, use_global_device_ids=true, to_apply=%region_8.9.clone | all-reduce | flops 512 | bytes 4096
  74.1 0.1 broadcast_in_dim.16
  74.2 0.1 reshape.84
  74.3 3.6 %all-to-all-start = ((bf16[4,128,512]{2,1,0:T(8,128)(2,1)}), bf16[4,128,512]{2,1,0:T(8,128)(2,1)S(1)}, u32[]{:S(2)}, u32[]{:S(2)}) async-start(bf16[4,128,512]{2,1,0:T(8,128)(2,1)} %bitcast.74), calls=%async_computation | async-start | bytes 1048576 | tf_op jit(solution)/shard_map/all_to_all | solution.py:65
  77.9 0.8 divide_convert_fusion
  78.6 0.0 copy-start.4
  78.6 4.4 %all_gather.14 = bf16[8,2048]{1,0:T(8,128)(2,1)S(1)} all-gather(bf16[8,1024]{1,0:T(8,128)(2,1)S(1)} %divide_convert_fusion), channel_id=1, replica_groups=mesh['clips'=2,'seq'=4,'tp'=2,'dp'=2] {'tp'}, dimensions={1}, use_global_device_ids=true | all-gather | bytes 49152 | tf_op jit(solution)/shard_map/all_gather | solution.py:109
  83.1 0.1 multiply_reduce_fusion
  83.2 0.1 fusion.50
  83.3 13.9 %all_gather.15 = bf16[32,1024]{1,0:T(8,128)(2,1)S(1)} all-gather(bf16[8,1024]{1,0:T(8,128)(2,1)S(1)} %fusion.50), channel_id=1, replica_groups=mesh['clips'=2,'seq'=4,'tp'=2,'dp'=2] {'seq'}, dimensions={0}, use_global_device_ids=true | all-gather | bytes 81920 | tf_op jit(solution)/shard_map/all_gather | solution.py:118
  97.2 4.6 %all-to-all-start.2 = ((bf16[4,128,512]{2,1,0:T(8,128)(2,1)}), bf16[4,128,512]{2,1,0:T(8,128)(2,1)S(1)}, u32[]{:S(2)}, u32[]{:S(2)}) async-start(bf16[4,128,512]{2,1,0:T(8,128)(2,1)} %bitcast.73), calls=%async_computation.2 | async-start | bytes 1048576 | tf_op jit(solution)/shard_map/all_to_all | solution.py:66
  101.7 3.7 %fusion.58 = f32[32,2048]{1,0:T(8,128)} fusion(bf16[32,1024]{1,0:T(8,128)(2,1)S(1)} %all_gather.15, bf16[1024,2048]{1,0:T(8,128)(2,1)} %param.24), kind=kOutput, calls=%fused_computation.76 | convolution fusion | flops 134217728 | bytes 4521984 | tf_op jit(solution)/shard_map/dot_general | solution.py:117
  105.4 0.0 all-reduce.3.cloned.1.call-update
  105.5 0.1 reshape.77
  105.6 0.1 reshape_reshape.10
  105.7 0.7 bitcast_reduce_fusion
  106.5 1.9 %copy-done = f32[4,512,512]{2,1,0:T(8,128)} copy-done((f32[4,512,512]{2,1,0:T(8,128)}, f32[4,512,512]{2,1,0:T(8,128)S(1)}, u32[]{:S(2)}) %copy-start) | copy-done | bytes 4194328
  108.4 0.7 fusion.1
  109.1 7.0 %all-to-all-done.2 = bf16[4,128,512]{2,1,0:T(8,128)(2,1)S(1)} async-done(((bf16[4,128,512]{2,1,0:T(8,128)(2,1)}), bf16[4,128,512]{2,1,0:T(8,128)(2,1)S(1)}, u32[]{:S(2)}, u32[]{:S(2)}) %all-to-all-start.2) | async-done | bytes 524320 | tf_op jit(solution)/shard_map/all_to_all | solution.py:66
  116.1 0.1 reshape_reshape.11
  116.2 3.4 %fusion.17 = bf16[512,4,128]{2,0,1:T(8,128)(2,1)S(1)} fusion(f32[4,512,512]{2,1,0:T(8,128)} %copy-done, f32[512,4]{0,1:T(4,128)S(1)} %get-tuple-element.52, bf16[512,4,128]{2,1,0:T(4,128)(2,1)S(1)} %reshape_reshape.11, f32[512,4]{0,1:T(4,128)S(1)} %fusion.1), kind=kOutput, calls=%fused_computation.18 | convolution fusion | flops 272105472 | bytes 5259264 | tf_op jit(solution)/shard_map/while/body/eval_jaxpr/qhk,khd->qhd/dot_general | solution.py:22
  119.6 0.4 copy.63
  120.0 1.0 convert_element_type.56
  121.0 3.5 %all-to-all-start.3 = ((bf16[4,128,512]{2,1,0:T(8,128)(2,1)}), bf16[4,128,512]{2,1,0:T(8,128)(2,1)S(1)}, u32[]{:S(2)}, u32[]{:S(2)}) async-start(bf16[4,128,512]{2,1,0:T(8,128)(2,1)} %convert_element_type.56), calls=%async_computation.3 | async-start | bytes 1048576 | tf_op jit(solution)/shard_map/all_to_all | solution.py:71
  124.5 0.0 reduce-scatter.5.cloned.1.call-start
  124.5 5.8 %all-reduce.3.cloned.1.call-done = f32[32,2048]{1,0:T(8,128)} async-done(((f32[32,2048]{1,0:T(8,128)}), f32[32,2048]{1,0:T(8,128)}) %all-reduce.3.cloned.1.call-update) | async-done | bytes 262160 | tf_op jit(solution)/shard_map/psum | solution.py:122
  130.4 3.7 %fusion.38 = f32[32,1024]{1,0:T(8,128)} fusion(bf16[2048,1024]{1,0:T(8,128)(2,1)} %param.25, f32[32,2048]{1,0:T(8,128)} %all-reduce.3.cloned.1.call-done), kind=kOutput, calls=%fused_computation.41 | convolution fusion | flops 134807552 | bytes 4587520 | tf_op jit(solution)/shard_map/dot_general | solution.py:124
  134.1 0.0 reduce-scatter.5.cloned.1.call-update
  134.1 13.3 %all-gather.1 = bf16[1,32,1024]{2,1,0:T(8,128)(2,1)S(1)} all-gather(bf16[1,8,1024]{2,1,0:T(8,128)(2,1)S(1)} %copy-done.7), channel_id=3, replica_groups=mesh['clips'=2,'seq'=4,'tp'=2,'dp'=2] {'seq'}, dimensions={1}, use_global_device_ids=true | all-gather | bytes 81920 | tf_op jit(solution)/shard_map/all_gather | solution.py:156
  147.4 0.1 reshape.81
  147.5 0.3 fusion.11
  147.8 0.9 copy.74
  148.7 5.2 %reduce-scatter.5.cloned.1.call-done = f32[8,1024]{1,0:T(8,128)} async-done(((f32[32,1024]{1,0:T(8,128)}), f32[8,1024]{1,0:T(8,128)}) %reduce-scatter.5.cloned.1.call-update) | async-done | bytes 32784 | tf_op jit(solution)/shard_map/reduce_scatter | solution.py:123
  153.8 1.4 convert_bitcast_fusion
  155.2 0.3 copy.64
  155.5 1.0 copy.73
  (37 shorter events, 0.1 us)
Async XLA Ops:
  7.2 34.9 %copy-start.5 = (bf16[1,8,1024]{2,1,0:T(8,128)(2,1)S(1)}, bf16[1,8,1024]{2,1,0:T(8,128)(2,1)}, u32[]{:S(2)}) copy-start(bf16[1,8,1024]{2,1,0:T(8,128)(2,1)} %param.19) | copy-start | bytes 49156
  7.2 31.5 %copy-start.3 = (bf16[1,128,1024]{2,1,0:T(8,128)(2,1)S(1)}, bf16[1,128,1024]{2,1,0:T(8,128)(2,1)}, u32[]{:S(2)}) copy-start(bf16[1,128,1024]{2,1,0:T(8,128)(2,1)} %param.20) | copy-start | bytes 786436
  7.2 46.1 %copy-start.1 = (bf16[1,128,2048]{2,1,0:T(8,128)(2,1)S(1)}, bf16[1,128,2048]{2,1,0:T(8,128)(2,1)}, u32[]{:S(2)}) copy-start(bf16[1,128,2048]{2,1,0:T(8,128)(2,1)} %param.14) | copy-start | bytes 1572868
  7.2 10.0 %collective-permute-start = (bf16[8,1024]{1,0:T(8,128)(2,1)}, bf16[8,1024]{1,0:T(8,128)(2,1)S(1)}, u32[]{:S(2)}, u32[]{:S(2)}) collective-permute-start(bf16[8,1024]{1,0:T(8,128)(2,1)} %bitcast.83), channel_id=1, source_target_pairs={{0,4},{4,8},{8,12},{12,0},{1,5},{5,9},{9,13},{13,1},{2,6},{6,10},{... | collective-permute-start | bytes 49160 | tf_op jit(solution)/shard_map/ppermute | solution.py:151
  12.2 62.1 %all-to-all-start.1 = ((bf16[4,128,512]{2,1,0:T(8,128)(2,1)}), bf16[4,128,512]{2,1,0:T(8,128)(2,1)S(1)}, u32[]{:S(2)}, u32[]{:S(2)}) async-start(bf16[4,128,512]{2,1,0:T(8,128)(2,1)} %bitcast.72), calls=%async_computation.1 | async-start | bytes 1048576 | tf_op jit(solution)/shard_map/all_to_all | solution.py:58
  16.0 38.6 %copy-start.2 = (bf16[1,128,2048]{2,1,0:T(8,128)(2,1)S(1)}, bf16[1,128,2048]{2,1,0:T(8,128)(2,1)}, u32[]{:S(2)}) copy-start(bf16[1,128,2048]{2,1,0:T(8,128)(2,1)} %param.15) | copy-start | bytes 1572868
  16.0 61.8 %reduce-scatter.3.cloned.1.call-start = ((), (), s32[]{:S(2)}) async-start(), calls=%async_computation.6 | async-start | bytes 163840 | tf_op jit(solution)/shard_map/reduce_scatter | solution.py:103
  17.2 19.2 %collective-permute-start.1 = (bf16[8,1024]{1,0:T(8,128)(2,1)S(1)}, bf16[8,1024]{1,0:T(8,128)(2,1)S(1)}, u32[]{:S(2)}, u32[]{:S(2)}) collective-permute-start(bf16[8,1024]{1,0:T(8,128)(2,1)S(1)} %collective-permute-done), channel_id=1, source_target_pairs={{0,4},{4,8},{8,12},{12,0},{1,5},{5,9},{9,13},{13,1},{2,6},{6,10},{... | collective-permute-start | bytes 49160 | tf_op jit(solution)/shard_map/ppermute | solution.py:151
  36.5 5.6 %collective-permute-start.2 = (bf16[8,1024]{1,0:T(8,128)(2,1)S(1)}, bf16[8,1024]{1,0:T(8,128)(2,1)S(1)}, u32[]{:S(2)}, u32[]{:S(2)}) collective-permute-start(bf16[8,1024]{1,0:T(8,128)(2,1)S(1)} %collective-permute-done.1), channel_id=1, source_target_pairs={{0,4},{4,8},{8,12},{12,0},{1,5},{5,9},{9,13},{13,1},{2,6},{6,10},{... | collective-permute-start | bytes 49160 | tf_op jit(solution)/shard_map/ppermute | solution.py:151
  38.7 17.2 %copy-start.9 = (u32[32]{0:T(128)S(1)}, u32[32]{0:T(128)}, u32[]{:S(2)}) copy-start(u32[32]{0:T(128)} %constant.105) | copy-start | bytes 388
  38.7 18.4 %copy-start.8 = (f32[2048]{0:T(1024)S(1)}, f32[2048]{0:T(1024)}, u32[]{:S(2)}) copy-start(f32[2048]{0:T(1024)} %param.23) | copy-start | bytes 24580
  42.6 40.5 %copy-start.6 = (bf16[1,8,2048]{2,1,0:T(8,128)(2,1)S(1)}, bf16[1,8,2048]{2,1,0:T(8,128)(2,1)}, u32[]{:S(2)}) copy-start(bf16[1,8,2048]{2,1,0:T(8,128)(2,1)} %param.22) | copy-start | bytes 98308
  74.3 22.9 %all-to-all-start = ((bf16[4,128,512]{2,1,0:T(8,128)(2,1)}), bf16[4,128,512]{2,1,0:T(8,128)(2,1)S(1)}, u32[]{:S(2)}, u32[]{:S(2)}) async-start(bf16[4,128,512]{2,1,0:T(8,128)(2,1)} %bitcast.74), calls=%async_computation | async-start | bytes 1048576 | tf_op jit(solution)/shard_map/all_to_all | solution.py:65
  78.6 27.8 %copy-start.4 = (bf16[8,1024]{1,0:T(8,128)(2,1)}, bf16[8,1024]{1,0:T(8,128)(2,1)S(1)}, u32[]{:S(2)}) copy-start(bf16[8,1024]{1,0:T(8,128)(2,1)S(1)} %divide_convert_fusion) | copy-start | bytes 49156
  97.2 18.9 %all-to-all-start.2 = ((bf16[4,128,512]{2,1,0:T(8,128)(2,1)}), bf16[4,128,512]{2,1,0:T(8,128)(2,1)S(1)}, u32[]{:S(2)}, u32[]{:S(2)}) async-start(bf16[4,128,512]{2,1,0:T(8,128)(2,1)} %bitcast.73), calls=%async_computation.2 | async-start | bytes 1048576 | tf_op jit(solution)/shard_map/all_to_all | solution.py:66
  101.7 28.6 %all-reduce.3.cloned.1.call-start = ((), (), s32[]{:S(2)}) async-start(), calls=%async_computation.7 | async-start | bytes 524288 | tf_op jit(solution)/shard_map/psum | solution.py:122
  106.5 1.9 %copy-start = (f32[4,512,512]{2,1,0:T(8,128)}, f32[4,512,512]{2,1,0:T(8,128)S(1)}, u32[]{:S(2)}) copy-start(f32[4,512,512]{2,1,0:T(8,128)S(1)} %get-tuple-element.53) | copy-start | bytes 12582916
  119.6 14.5 %copy-start.7 = (bf16[1,8,1024]{2,1,0:T(8,128)(2,1)S(1)}, bf16[1,8,1024]{2,1,0:T(8,128)(2,1)}, u32[]{:S(2)}) copy-start(bf16[1,8,1024]{2,1,0:T(8,128)(2,1)} %param.18) | copy-start | bytes 49156
  121.0 34.2 %all-to-all-start.3 = ((bf16[4,128,512]{2,1,0:T(8,128)(2,1)}), bf16[4,128,512]{2,1,0:T(8,128)(2,1)S(1)}, u32[]{:S(2)}, u32[]{:S(2)}) async-start(bf16[4,128,512]{2,1,0:T(8,128)(2,1)} %convert_element_type.56), calls=%async_computation.3 | async-start | bytes 1048576 | tf_op jit(solution)/shard_map/all_to_all | solution.py:71
  124.5 29.3 %reduce-scatter.5.cloned.1.call-start = ((), (), s32[]{:S(2)}) async-start(), calls=%async_computation.8 | async-start | bytes 163840 | tf_op jit(solution)/shard_map/reduce_scatter | solution.py:123
Sparse Core Ops, SparseCore 0:
  53.4 18.2 reduce-scatter.2
  105.6 24.7 all-reduce.2
  134.2 19.5 reduce-scatter.4
